TPU v7x, 128 devices: a whole 4x4x4 slice. The times are simulated.
128 devices in a mesh: sub: 16 (over z, x), grp: 8 (over y, core).
Axes of the slice: x: 4, y: 4, z: 4, core: 2. Of those that a mesh axis runs over, the one named last changes fastest.
Arguments:
- rhs: float32 [8, 64, 256, 256], P('grp', 'sub')
- counts: int32 [8, 64], P('grp', 'sub'), may hold values from 64 to 256, as said below
- solve_panel: bfloat16 [8, 64, 512, 512], P('grp', 'sub'), as said below
- dirichlet_panel: bfloat16 [8, 64, 512, 512], P('grp', 'sub'), as said below
- coupling: float32 [8, 64, 32, 512], P('grp', 'sub'), may hold values from -0.25 to 0.25
- corner_map: int32 [8, 64, 32], P('grp', 'sub'), may hold values from 0 to 2047
- coarse_inverse: float32 [16, 2048, 2048], P('sub', 'grp'), as said below
Outputs:
- multipliers: float32 [8, 64, 256, 256], P('grp', 'sub')
- residual: float32 [8, 64, 256, 256], P('grp', 'sub')
Inputs may be any that keep to these rules, and one draw needn't show every extreme that they name: `counts`: some pair has all 256 unknowns constrained. `solve_panel`: each panel is symmetric positive definite. `dirichlet_panel`: each panel is symmetric positive definite. `coarse_inverse`: each slab's matrix is symmetric positive definite.
All inputs are finite; a program needn't handle non-finite values.
Results may differ from a plain program's by a relative error of at most 0.0003.
Values sent between devices are 32-bit elements; how exact they have to be, the bound alone decides.
A program may use at most 128 MiB of HBM per device.

v0:
```python
import jax
import jax.numpy as jnp
from jax import lax
from jax.sharding import PartitionSpec as P

ITERS = 3
HIGH = lax.Precision.HIGHEST


def passed_along(block, axis, distance):
    devices = range(lax.axis_size(axis))
    route = [(i - distance, i) for i in devices if i - distance in devices]
    return lax.ppermute(block, axis, route)


def spread_faces(values):
    previous = passed_along(values[:, -1:], "sub", 1)
    prior = jnp.concatenate([previous, values[:, :-1]], axis=1)
    return jnp.concatenate([-prior, values], axis=3)


def face_jump(result, live_mask):
    width = result.shape[3] // 2
    following = passed_along(result[:, :1, :, :width], "sub", -1)
    next_left = jnp.concatenate([result[:, 1:, :, :width], following], axis=1)
    return live_mask * (result[..., width:] - next_left)


def panel_apply(panel, face_vals):
    return jnp.einsum(
        "gsrp,gsqp->gsrq", face_vals, panel, precision=HIGH, preferred_element_type=jnp.float32
    )


def inner(first, second):
    return jnp.sum(first * second, axis=(0, 1, 3))


def expand(scalars):
    return scalars[None, None, :, None]


def residual_sum(resid, precond):
    return lax.psum(inner(resid, precond), ("sub", "grp"))


def local(rhs, counts, solve_panel, dirichlet_panel, coupling, corner_map, coarse_inverse):
    local_subs = rhs.shape[1]
    width = rhs.shape[3]
    size = coarse_inverse.shape[2]
    last_device = lax.axis_index("sub") == lax.axis_size("sub") - 1
    slots = jnp.arange(local_subs, dtype=jnp.int32)
    positions = jnp.arange(width, dtype=jnp.int32)
    not_last = jnp.logical_not(last_device & (slots == local_subs - 1))
    live = (positions[None, None, :] < counts[:, :, None]) & not_last[None, :, None]
    live_mask = live.astype(jnp.float32)[:, :, None, :]
    corner_onehot = (corner_map[0][..., None] == jnp.arange(size, dtype=jnp.int32)).astype(
        jnp.float32
    )

    def precondition(values):
        return 0.25 * face_jump(panel_apply(dirichlet_panel, spread_faces(values)), live_mask)

    multipliers = jnp.zeros_like(rhs)
    residual = live_mask * rhs
    precond = precondition(residual)
    direction = precond
    rz_now = residual_sum(residual, precond)
    for step in range(ITERS):
        apply_face_vals = spread_faces(direction)
        corner_vals = jnp.einsum("srp,skp->srk", apply_face_vals[0], coupling[0], precision=HIGH)
        owned_totals = lax.psum_scatter(
            jnp.einsum("skn,srk->nr", corner_onehot, corner_vals, precision=HIGH),
            "grp",
            scatter_dimension=0,
            tiled=True,
        )
        partial_solved = jnp.einsum("mn,mr->nr", coarse_inverse[0], owned_totals, precision=HIGH)
        solved = lax.psum(partial_solved, "grp")
        back = jnp.einsum("skn,nr->srk", corner_onehot, solved, precision=HIGH)
        result = (
            panel_apply(solve_panel, apply_face_vals)
            + jnp.einsum("srk,skp->srp", back, coupling[0], precision=HIGH)[None]
        )
        image = face_jump(result, live_mask)
        alpha = rz_now / lax.psum(inner(direction, image), ("sub", "grp"))
        multipliers = multipliers + expand(alpha) * direction
        residual = residual - expand(alpha) * image
        if step + 1 < ITERS:
            precond = precondition(residual)
            rz_next = residual_sum(residual, precond)
            direction = precond + expand(rz_next / rz_now) * direction
            rz_now = rz_next
    return (multipliers, residual)


def solution(mesh):
    return jax.shard_map(
        local,
        mesh=mesh,
        in_specs=(
            P("grp", "sub", None, None),
            P("grp", "sub"),
            P("grp", "sub", None, None),
            P("grp", "sub", None, None),
            P("grp", "sub", None, None),
            P("grp", "sub", None),
            P("sub", "grp", None),
        ),
        out_specs=(P("grp", "sub", None, None), P("grp", "sub", None, None)),
        check_vma=False,
    )
```

profile of v0, /device:TPU:1, one launch (start us, length us, event | category | flops | bytes accessed | tf_op | source)
XLA Modules:
  0.0 832.8 jit_solution(642383770802080915)
XLA Ops:
  13.5 4.9 collective-permute-done
  21.7 7.8 collective-permute-done.1
  42.0 38.6 %reduce-scatter.4.cloned.1.call-done = f32[256,256]{1,0:T(8,128)} async-done(((f32[2048,256]{1,0:T(8,128)}), f32[256,256]{1,0:T(8,128)}) %reduce-scatter.4.cloned.1.call-update) | async-done | bytes 262160 | tf_op jit(solution)/shard_map/reduce_scatter | solution.py:72
  80.6 4.9 convolution_bitcast_fusion.5
  85.8 65.4 %all-reduce.5.cloned.1.call-done = f32[2048,256]{0,1:T(8,128)} async-done(((f32[2048,256]{0,1:T(8,128)}), f32[2048,256]{0,1:T(8,128)}) %all-reduce.5.cloned.1.call-update) | async-done | bytes 2097168 | tf_op jit(solution)/shard_map/psum | solution.py:79
  159.7 5.7 collective-permute-done.3
  166.2 70.6 %all-reduce = (f32[256]{0:T(256)S(1)}, f32[256]{0:T(256)S(1)}) all-reduce(f32[256]{0:T(256)S(1)} %get-tuple-element.3, f32[256]{0:T(256)S(1)} %get-tuple-element.2), channel_id=1, replica_groups=mesh['sub'=16,'grp'=8] {'sub','grp'}, use_global_device_ids=true, to_apply=%region_1.0 | all-reduce | flops 512 | bytes 4096 | tf_op jit(solution)/shard_map/psum | solution.py:44
  241.4 4.6 collective-permute-done.4
  249.4 7.5 collective-permute-done.5
  258.0 67.7 %psum.66 = f32[256]{0:T(256)S(1)} all-reduce(f32[256]{0:T(256)S(1)} %multiply_reduce_fusion.3), channel_id=1, replica_groups=mesh['sub'=16,'grp'=8] {'sub','grp'}, use_global_device_ids=true, to_apply=%region_7.0 | all-reduce | flops 256 | bytes 2048 | tf_op jit(solution)/shard_map/psum | solution.py:44
  341.7 32.0 %reduce-scatter.6.cloned.1.call-done = f32[256,256]{1,0:T(8,128)} async-done(((f32[2048,256]{1,0:T(8,128)}), f32[256,256]{1,0:T(8,128)}) %reduce-scatter.6.cloned.1.call-update) | async-done | bytes 262160 | tf_op jit(solution)/shard_map/reduce_scatter | solution.py:72
  373.7 4.9 convolution_bitcast_fusion.4
  378.7 65.6 %all-reduce.7.cloned.1.call-done = f32[2048,256]{0,1:T(8,128)} async-done(((f32[2048,256]{0,1:T(8,128)}), f32[2048,256]{0,1:T(8,128)}) %all-reduce.7.cloned.1.call-update) | async-done | bytes 2097168 | tf_op jit(solution)/shard_map/psum | solution.py:79
  452.6 5.7 collective-permute-done.7
  459.4 71.1 %psum.68 = f32[256]{0:T(256)S(1)} all-reduce(f32[256]{0:T(256)S(1)} %multiply_reduce_fusion.2), channel_id=1, replica_groups=mesh['sub'=16,'grp'=8] {'sub','grp'}, use_global_device_ids=true, to_apply=%region_11.0 | all-reduce | flops 256 | bytes 2048 | tf_op jit(solution)/shard_map/psum | solution.py:86
  535.1 4.6 collective-permute-done.8
  543.0 7.5 collective-permute-done.9
  551.6 67.7 %psum.69 = f32[256]{0:T(256)S(1)} all-reduce(f32[256]{0:T(256)S(1)} %multiply_reduce_fusion.1), channel_id=1, replica_groups=mesh['sub'=16,'grp'=8] {'sub','grp'}, use_global_device_ids=true, to_apply=%region_13.0 | all-reduce | flops 256 | bytes 2048 | tf_op jit(solution)/shard_map/psum | solution.py:44
  623.6 4.8 collective-permute-done.10
  634.3 31.8 %reduce-scatter.8.cloned.1.call-done = f32[256,256]{1,0:T(8,128)} async-done(((f32[2048,256]{1,0:T(8,128)}), f32[256,256]{1,0:T(8,128)}) %reduce-scatter.8.cloned.1.call-update) | async-done | bytes 262160 | tf_op jit(solution)/shard_map/reduce_scatter | solution.py:72
  666.1 4.9 convolution_bitcast_fusion.3
  671.0 65.7 %all-reduce.9.cloned.1.call-done = f32[2048,256]{0,1:T(8,128)} async-done(((f32[2048,256]{0,1:T(8,128)}), f32[2048,256]{0,1:T(8,128)}) %all-reduce.9.cloned.1.call-update) | async-done | bytes 2097168 | tf_op jit(solution)/shard_map/psum | solution.py:79
  744.9 5.7 collective-permute-done.11
  750.9 70.7 %psum.71 = f32[256]{0:T(256)S(1)} all-reduce(f32[256]{0:T(256)S(1)} %multiply_reduce_fusion), channel_id=1, replica_groups=mesh['sub'=16,'grp'=8] {'sub','grp'}, use_global_device_ids=true, to_apply=%region_17.0 | all-reduce | flops 256 | bytes 2048 | tf_op jit(solution)/shard_map/psum | solution.py:86
  (161 shorter events, 97.1 us)
Async XLA Ops:
  7.2 11.3 %copy-start = (bf16[1,4,512,512]{3,2,1,0:T(8,128)(2,1)S(1)}, bf16[1,4,512,512]{3,2,1,0:T(8,128)(2,1)}, u32[]{:S(2)}) copy-start(bf16[1,4,512,512]{3,2,1,0:T(8,128)(2,1)} %param.10) | copy-start | bytes 6291460
  7.2 73.4 %reduce-scatter.4.cloned.1.call-start = ((), (), s32[]{:S(2)}) async-start(), calls=%async_computation.3 | async-start | bytes 2359296 | tf_op jit(solution)/shard_map/reduce_scatter | solution.py:72
  9.4 8.9 %collective-permute-start = (f32[1,1,256,256]{3,2,1,0:T(8,128)S(1)}, f32[1,1,256,256]{3,2,1,0:T(8,128)S(1)}, u32[]{:S(2)}, u32[]{:S(2)}) collective-permute-start(f32[1,1,256,256]{3,2,1,0:T(8,128)S(1)} %slice.120), channel_id=1, source_target_pairs={{0,8},{8,16},{16,24},{24,32},{32,40},{40,48},{48,56},{56,64},{64,7... | collective-permute-start | bytes 786440 | tf_op jit(solution)/shard_map/ppermute | solution.py:13
  20.3 9.2 %collective-permute-start.1 = (f32[1,1,256,256]{3,2,1,0:T(8,128)S(1)}, f32[1,1,256,256]{3,2,1,0:T(8,128)S(1)}, u32[]{:S(2)}, u32[]{:S(2)}) collective-permute-start(f32[1,1,256,256]{3,2,1,0:T(8,128)S(1)} %slice.124), channel_id=1, source_target_pairs={{8,0},{16,8},{24,16},{32,24},{40,32},{48,40},{56,48},{64,56},{72,6... | collective-permute-start | bytes 786440 | tf_op jit(solution)/shard_map/ppermute | solution.py:13
  29.7 135.8 %copy-start.8 = (f32[1,4,256,256]{3,2,1,0:T(8,128)}, f32[1,4,256,256]{3,2,1,0:T(8,128)S(1)}, u32[]{:S(2)}) copy-start(f32[1,4,256,256]{3,2,1,0:T(8,128)S(1)} %get-tuple-element.9) | copy-start | bytes 3145732
  29.7 6.5 collective-permute-start.2
  42.0 109.2 %all-reduce.5.cloned.1.call-start = ((), (), s32[]{:S(2)}) async-start(), calls=%async_computation.4 | async-start | bytes 4194304 | tf_op jit(solution)/shard_map/psum | solution.py:79
  85.5 288.2 %reduce-scatter.6.cloned.1.call-start = ((), (), s32[]{:S(2)}) async-start(), calls=%async_computation.5 | async-start | bytes 2359296 | tf_op jit(solution)/shard_map/reduce_scatter | solution.py:72
  158.1 7.4 collective-permute-start.3
  238.9 18.0 %copy-start.4 = (f32[1,4,256,256]{3,2,1,0:T(8,128)}, f32[1,4,256,256]{3,2,1,0:T(8,128)S(1)}, u32[]{:S(2)}) copy-start(f32[1,4,256,256]{3,2,1,0:T(8,128)S(1)} %multiply_subtract_fusion.2) | copy-start | bytes 3145732
  238.9 7.1 collective-permute-start.4
  248.0 8.9 %copy-start.11 = (f32[1,4,256,512]{3,2,1,0:T(8,128)}, f32[1,4,256,512]{3,2,1,0:T(8,128)S(1)}, u32[]{:S(2)}) copy-start(f32[1,4,256,512]{3,2,1,0:T(8,128)S(1)} %fusion.39) | copy-start | bytes 6291460
  248.0 8.9 %collective-permute-start.5 = (f32[1,1,256,256]{3,2,1,0:T(8,128)S(1)}, f32[1,1,256,256]{3,2,1,0:T(8,128)S(1)}, u32[]{:S(2)}, u32[]{:S(2)}) collective-permute-start(f32[1,1,256,256]{3,2,1,0:T(8,128)S(1)} %slice.134), channel_id=1, source_target_pairs={{8,0},{16,8},{24,16},{32,24},{40,32},{48,40},{56,48},{64,56},{72,6... | collective-permute-start | bytes 786440 | tf_op jit(solution)/shard_map/ppermute | solution.py:13
  327.8 7.2 collective-permute-start.6
  341.7 102.7 %all-reduce.7.cloned.1.call-start = ((), (), s32[]{:S(2)}) async-start(), calls=%async_computation.6 | async-start | bytes 4194304 | tf_op jit(solution)/shard_map/psum | solution.py:79
  378.7 287.4 %reduce-scatter.8.cloned.1.call-start = ((), (), s32[]{:S(2)}) async-start(), calls=%async_computation.7 | async-start | bytes 2359296 | tf_op jit(solution)/shard_map/reduce_scatter | solution.py:72
  451.2 7.1 collective-permute-start.7
  532.5 18.0 %copy-start.3 = (f32[1,4,256,256]{3,2,1,0:T(8,128)}, f32[1,4,256,256]{3,2,1,0:T(8,128)S(1)}, u32[]{:S(2)}) copy-start(f32[1,4,256,256]{3,2,1,0:T(8,128)S(1)} %multiply_subtract_fusion.1) | copy-start | bytes 3145732
  532.6 7.1 collective-permute-start.8
  541.6 8.9 %copy-start.12 = (f32[1,4,256,512]{3,2,1,0:T(8,128)}, f32[1,4,256,512]{3,2,1,0:T(8,128)S(1)}, u32[]{:S(2)}) copy-start(f32[1,4,256,512]{3,2,1,0:T(8,128)S(1)} %fusion.36) | copy-start | bytes 6291460
  541.6 8.9 %collective-permute-start.9 = (f32[1,1,256,256]{3,2,1,0:T(8,128)S(1)}, f32[1,1,256,256]{3,2,1,0:T(8,128)S(1)}, u32[]{:S(2)}, u32[]{:S(2)}) collective-permute-start(f32[1,1,256,256]{3,2,1,0:T(8,128)S(1)} %slice.144), channel_id=1, source_target_pairs={{8,0},{16,8},{24,16},{32,24},{40,32},{48,40},{56,48},{64,56},{72,6... | collective-permute-start | bytes 786440 | tf_op jit(solution)/shard_map/ppermute | solution.py:13
  621.1 7.2 collective-permute-start.10
  634.1 102.6 %all-reduce.9.cloned.1.call-start = ((), (), s32[]{:S(2)}) async-start(), calls=%async_computation.8 | async-start | bytes 4194304 | tf_op jit(solution)/shard_map/psum | solution.py:79
  743.6 7.1 collective-permute-start.11
  (28 other events, 135.8 us)
Sparse Core Ops, SparseCore 0:
  42.1 38.4 reduce-scatter.3
  85.7 65.4 all-reduce.4
  341.8 31.8 reduce-scatter.5
  378.8 65.5 all-reduce.6
  634.2 31.8 reduce-scatter.7
  671.1 65.4 all-reduce.8
where the time goes:
time: 841 us; the launch traced here: 833 us
  waiting for transfers between devices  366 us (44%)
  blocking collectives  348 us (41%)
  matrix products  57.2 us (7%)
  starting transfers between devices  25.7 us (3%)
  other arithmetic  16.7 us (2%)
  between operations  15.2 us (2%)
    psum x3, blocking collectives, residual_sum(): return lax.psum(inner(resid, precond), ('sub', 'grp'))  206 us
    psum x3, waiting for transfers between devices, local(): solved = lax.psum(partial_solved, 'grp')  197 us
    psum x2, blocking collectives, local(): alpha = rz_now / lax.psum(inner(direction, image), ('sub', 'grp'))  142 us
    reduce_scatter x3, waiting for transfers between devices, local(): lax.psum_scatter(jnp.einsum('skn,srk->nr', corner_onehot, corner_vals, pr...  102 us
    ppermute x12, waiting for transfers between devices, passed_along(): return lax.ppermute(block, axis, route)  66.6 us
    ppermute x12, starting transfers between devices, passed_along(): return lax.ppermute(block, axis, route)  25.1 us
  transfers between devices with their start and end apart: 18, of which 18 were waited for; matrix products, arithmetic and copies ran while one was open for 0% of the time, Pallas kernels for 0%

commit v1 on v0

--- a/solution.py
+++ b/solution.py
@@ -2,6 +2,7 @@
 import jax.numpy as jnp
 from jax import lax
 from jax.sharding import PartitionSpec as P
+from jax.lax import psum
 
 ITERS = 3
 HIGH = lax.Precision.HIGHEST
@@ -41,7 +42,7 @@
 
 
 def residual_sum(resid, precond):
-    return lax.psum(inner(resid, precond), ("sub", "grp"))
+    return psum(psum(inner(resid, precond), "sub"), "grp")
 
 
 def local(rhs, counts, solve_panel, dirichlet_panel, coupling, corner_map, coarse_inverse):

time: 841 us -> 851 us (1.012)
  blocking collectives: 348 us -> 366 us
    psum x2 -> x3, blocking collectives: 142 us -> 212 us  [local(): alpha = rz_now / lax.psum(inner(direction, image), ('sub', 'grp'))]
    psum x3 -> x6, blocking collectives: 206 us -> 153 us  [residual_sum(): return psum(psum(inner(resid, precond), 'sub'), 'grp')]
where the time goes in v1:
time: 851 us; the launch traced here: 844 us
  blocking collectives  366 us (43%)
  waiting for transfers between devices  361 us (42%)
  matrix products  57.2 us (7%)
  starting transfers between devices  23.4 us (3%)
  other arithmetic  16.7 us (2%)
  between operations  15.4 us (2%)
    psum x3, blocking collectives, local(): alpha = rz_now / lax.psum(inner(direction, image), ('sub', 'grp'))  212 us
    psum x3, waiting for transfers between devices, local(): solved = lax.psum(partial_solved, 'grp')  197 us
    psum x6, blocking collectives, residual_sum(): return psum(psum(inner(resid, precond), 'sub'), 'grp')  153 us
    reduce_scatter x3, waiting for transfers between devices, local(): lax.psum_scatter(jnp.einsum('skn,srk->nr', corner_onehot, corner_vals, pr...  96.2 us
    ppermute x12, waiting for transfers between devices, passed_along(): return lax.ppermute(block, axis, route)  68.3 us
    ppermute x12, starting transfers between devices, passed_along(): return lax.ppermute(block, axis, route)  22.4 us
  transfers between devices with their start and end apart: 18, of which 18 were waited for; matrix products, arithmetic and copies ran while one was open for 0% of the time, Pallas kernels for 0%

profile of v1, /device:TPU:1, one launch (start us, length us, event | category | flops | bytes accessed | tf_op | source)
XLA Modules:
  0.0 843.9 jit_solution(2750090977817290234)
XLA Ops:
  21.7 7.8 collective-permute-done.1
  42.1 38.5 %reduce-scatter.4.cloned.1.call-done = f32[256,256]{1,0:T(8,128)} async-done(((f32[2048,256]{1,0:T(8,128)}), f32[256,256]{1,0:T(8,128)}) %reduce-scatter.4.cloned.1.call-update) | async-done | bytes 262160 | tf_op jit(solution)/shard_map/reduce_scatter | solution.py:73
  80.5 4.9 convolution_bitcast_fusion.5
  86.0 65.2 %all-reduce.4.cloned.1.call-done = f32[2048,256]{0,1:T(8,128)} async-done(((f32[2048,256]{0,1:T(8,128)}), f32[2048,256]{0,1:T(8,128)}) %all-reduce.4.cloned.1.call-update) | async-done | bytes 2097168 | tf_op jit(solution)/shard_map/psum | solution.py:80
  159.8 5.7 collective-permute-done.3
  166.2 70.6 %psum.87 = f32[256]{0:T(256)S(1)} all-reduce(f32[256]{0:T(256)S(1)} %get-tuple-element.2), channel_id=1, replica_groups=mesh['sub'=16,'grp'=8] {'sub','grp'}, use_global_device_ids=true, to_apply=%region_6.0 | all-reduce | flops 256 | bytes 2048 | tf_op jit(solution)/shard_map/psum | solution.py:87
  236.8 30.8 %psum.84 = f32[256]{0:T(256)S(1)} all-reduce(f32[256]{0:T(256)S(1)} %get-tuple-element.3), channel_id=1, replica_groups=mesh['sub'=16,'grp'=8] {'sub'}, use_global_device_ids=true, to_apply=%region_1.0 | all-reduce | flops 256 | bytes 2048 | tf_op jit(solution)/shard_map/psum | solution.py:45
  267.7 19.6 %psum.85 = f32[256]{0:T(256)S(1)} all-reduce(f32[256]{0:T(256)S(1)} %psum.84), channel_id=1, replica_groups=mesh['sub'=16,'grp'=8] {'grp'}, use_global_device_ids=true, to_apply=%region_2.0 | all-reduce | flops 256 | bytes 2048 | tf_op jit(solution)/shard_map/psum | solution.py:45
  290.9 5.2 collective-permute-done.4
  299.4 8.2 collective-permute-done.5
  308.6 29.7 %psum.88 = f32[256]{0:T(256)S(1)} all-reduce(f32[256]{0:T(256)S(1)} %multiply_reduce_fusion.3), channel_id=1, replica_groups=mesh['sub'=16,'grp'=8] {'sub'}, use_global_device_ids=true, to_apply=%region_8.0 | all-reduce | flops 256 | bytes 2048 | tf_op jit(solution)/shard_map/psum | solution.py:45
  338.3 21.1 %psum.89 = f32[256]{0:T(256)S(1)} all-reduce(f32[256]{0:T(256)S(1)} %psum.88), channel_id=1, replica_groups=mesh['sub'=16,'grp'=8] {'grp'}, use_global_device_ids=true, to_apply=%region_9.0 | all-reduce | flops 256 | bytes 2048 | tf_op jit(solution)/shard_map/psum | solution.py:45
  375.1 27.7 %reduce-scatter.6.cloned.1.call-done = f32[256,256]{1,0:T(8,128)} async-done(((f32[2048,256]{1,0:T(8,128)}), f32[256,256]{1,0:T(8,128)}) %reduce-scatter.6.cloned.1.call-update) | async-done | bytes 262160 | tf_op jit(solution)/shard_map/reduce_scatter | solution.py:73
  407.8 65.6 %all-reduce.6.cloned.1.call-done = f32[2048,256]{0,1:T(8,128)} async-done(((f32[2048,256]{0,1:T(8,128)}), f32[2048,256]{0,1:T(8,128)}) %all-reduce.6.cloned.1.call-update) | async-done | bytes 2097168 | tf_op jit(solution)/shard_map/psum | solution.py:80
  481.7 5.7 collective-permute-done.7
  488.4 70.9 %psum.91 = f32[256]{0:T(256)S(1)} all-reduce(f32[256]{0:T(256)S(1)} %multiply_reduce_fusion.2), channel_id=1, replica_groups=mesh['sub'=16,'grp'=8] {'sub','grp'}, use_global_device_ids=true, to_apply=%region_13.0 | all-reduce | flops 256 | bytes 2048 | tf_op jit(solution)/shard_map/psum | solution.py:87
  571.9 7.5 collective-permute-done.9
  580.5 30.7 %psum.92 = f32[256]{0:T(256)S(1)} all-reduce(f32[256]{0:T(256)S(1)} %multiply_reduce_fusion.1), channel_id=1, replica_groups=mesh['sub'=16,'grp'=8] {'sub'}, use_global_device_ids=true, to_apply=%region_15.0 | all-reduce | flops 256 | bytes 2048 | tf_op jit(solution)/shard_map/psum | solution.py:45
  611.2 21.4 %psum.93 = f32[256]{0:T(256)S(1)} all-reduce(f32[256]{0:T(256)S(1)} %psum.92), channel_id=1, replica_groups=mesh['sub'=16,'grp'=8] {'grp'}, use_global_device_ids=true, to_apply=%region_16.0 | all-reduce | flops 256 | bytes 2048 | tf_op jit(solution)/shard_map/psum | solution.py:45
  635.8 5.0 collective-permute-done.10
  646.8 30.1 %reduce-scatter.8.cloned.1.call-done = f32[256,256]{1,0:T(8,128)} async-done(((f32[2048,256]{1,0:T(8,128)}), f32[256,256]{1,0:T(8,128)}) %reduce-scatter.8.cloned.1.call-update) | async-done | bytes 262160 | tf_op jit(solution)/shard_map/reduce_scatter | solution.py:73
  681.8 65.8 %all-reduce.8.cloned.1.call-done = f32[2048,256]{0,1:T(8,128)} async-done(((f32[2048,256]{0,1:T(8,128)}), f32[2048,256]{0,1:T(8,128)}) %all-reduce.8.cloned.1.call-update) | async-done | bytes 2097168 | tf_op jit(solution)/shard_map/psum | solution.py:80
  755.8 5.7 collective-permute-done.11
  761.8 70.7 %psum.95 = f32[256]{0:T(256)S(1)} all-reduce(f32[256]{0:T(256)S(1)} %multiply_reduce_fusion), channel_id=1, replica_groups=mesh['sub'=16,'grp'=8] {'sub','grp'}, use_global_device_ids=true, to_apply=%region_20.0 | all-reduce | flops 256 | bytes 2048 | tf_op jit(solution)/shard_map/psum | solution.py:87
  (165 shorter events, 114.3 us)
Async XLA Ops:
  7.2 11.3 %copy-start = (bf16[1,4,512,512]{3,2,1,0:T(8,128)(2,1)S(1)}, bf16[1,4,512,512]{3,2,1,0:T(8,128)(2,1)}, u32[]{:S(2)}) copy-start(bf16[1,4,512,512]{3,2,1,0:T(8,128)(2,1)} %param.10) | copy-start | bytes 6291460
  7.2 73.4 %reduce-scatter.4.cloned.1.call-start = ((), (), s32[]{:S(2)}) async-start(), calls=%async_computation.3 | async-start | bytes 2359296 | tf_op jit(solution)/shard_map/reduce_scatter | solution.py:73
  9.4 8.9 %collective-permute-start = (f32[1,1,256,256]{3,2,1,0:T(8,128)S(1)}, f32[1,1,256,256]{3,2,1,0:T(8,128)S(1)}, u32[]{:S(2)}, u32[]{:S(2)}) collective-permute-start(f32[1,1,256,256]{3,2,1,0:T(8,128)S(1)} %slice.120), channel_id=1, source_target_pairs={{0,8},{8,16},{16,24},{24,32},{32,40},{40,48},{48,56},{56,64},{64,7... | collective-permute-start | bytes 786440 | tf_op jit(solution)/shard_map/ppermute | solution.py:14
  20.3 9.2 %collective-permute-start.1 = (f32[1,1,256,256]{3,2,1,0:T(8,128)S(1)}, f32[1,1,256,256]{3,2,1,0:T(8,128)S(1)}, u32[]{:S(2)}, u32[]{:S(2)}) collective-permute-start(f32[1,1,256,256]{3,2,1,0:T(8,128)S(1)} %slice.124), channel_id=1, source_target_pairs={{8,0},{16,8},{24,16},{32,24},{40,32},{48,40},{56,48},{64,56},{72,6... | collective-permute-start | bytes 786440 | tf_op jit(solution)/shard_map/ppermute | solution.py:14
  29.7 135.8 %copy-start.8 = (f32[1,4,256,256]{3,2,1,0:T(8,128)}, f32[1,4,256,256]{3,2,1,0:T(8,128)S(1)}, u32[]{:S(2)}) copy-start(f32[1,4,256,256]{3,2,1,0:T(8,128)S(1)} %get-tuple-element.7) | copy-start | bytes 3145732
  29.8 6.5 collective-permute-start.2
  42.0 109.2 %all-reduce.4.cloned.1.call-start = ((), (), s32[]{:S(2)}) async-start(), calls=%async_computation.4 | async-start | bytes 4194304 | tf_op jit(solution)/shard_map/psum | solution.py:80
  85.5 317.3 %reduce-scatter.6.cloned.1.call-start = ((), (), s32[]{:S(2)}) async-start(), calls=%async_computation.5 | async-start | bytes 2359296 | tf_op jit(solution)/shard_map/reduce_scatter | solution.py:73
  158.1 7.4 collective-permute-start.3
  289.4 18.2 %copy-start.4 = (f32[1,4,256,256]{3,2,1,0:T(8,128)}, f32[1,4,256,256]{3,2,1,0:T(8,128)S(1)}, u32[]{:S(2)}) copy-start(f32[1,4,256,256]{3,2,1,0:T(8,128)S(1)} %multiply_subtract_fusion.2) | copy-start | bytes 3145732
  289.5 6.6 collective-permute-start.4
  298.0 9.6 %copy-start.11 = (f32[1,4,256,512]{3,2,1,0:T(8,128)}, f32[1,4,256,512]{3,2,1,0:T(8,128)S(1)}, u32[]{:S(2)}) copy-start(f32[1,4,256,512]{3,2,1,0:T(8,128)S(1)} %fusion.39) | copy-start | bytes 6291460
  298.0 9.5 %collective-permute-start.5 = (f32[1,1,256,256]{3,2,1,0:T(8,128)S(1)}, f32[1,1,256,256]{3,2,1,0:T(8,128)S(1)}, u32[]{:S(2)}, u32[]{:S(2)}) collective-permute-start(f32[1,1,256,256]{3,2,1,0:T(8,128)S(1)} %slice.134), channel_id=1, source_target_pairs={{8,0},{16,8},{24,16},{32,24},{40,32},{48,40},{56,48},{64,56},{72,6... | collective-permute-start | bytes 786440 | tf_op jit(solution)/shard_map/ppermute | solution.py:14
  361.5 6.9 collective-permute-start.6
  375.1 98.3 %all-reduce.6.cloned.1.call-start = ((), (), s32[]{:S(2)}) async-start(), calls=%async_computation.6 | async-start | bytes 4194304 | tf_op jit(solution)/shard_map/psum | solution.py:80
  407.7 269.1 %reduce-scatter.8.cloned.1.call-start = ((), (), s32[]{:S(2)}) async-start(), calls=%async_computation.7 | async-start | bytes 2359296 | tf_op jit(solution)/shard_map/reduce_scatter | solution.py:73
  480.3 7.1 collective-permute-start.7
  561.4 18.0 %copy-start.3 = (f32[1,4,256,256]{3,2,1,0:T(8,128)}, f32[1,4,256,256]{3,2,1,0:T(8,128)S(1)}, u32[]{:S(2)}) copy-start(f32[1,4,256,256]{3,2,1,0:T(8,128)S(1)} %multiply_subtract_fusion.1) | copy-start | bytes 3145732
  561.4 7.1 collective-permute-start.8
  570.5 8.9 %copy-start.12 = (f32[1,4,256,512]{3,2,1,0:T(8,128)}, f32[1,4,256,512]{3,2,1,0:T(8,128)S(1)}, u32[]{:S(2)}) copy-start(f32[1,4,256,512]{3,2,1,0:T(8,128)S(1)} %fusion.36) | copy-start | bytes 6291460
  570.5 8.9 %collective-permute-start.9 = (f32[1,1,256,256]{3,2,1,0:T(8,128)S(1)}, f32[1,1,256,256]{3,2,1,0:T(8,128)S(1)}, u32[]{:S(2)}, u32[]{:S(2)}) collective-permute-start(f32[1,1,256,256]{3,2,1,0:T(8,128)S(1)} %slice.144), channel_id=1, source_target_pairs={{8,0},{16,8},{24,16},{32,24},{40,32},{48,40},{56,48},{64,56},{72,6... | collective-permute-start | bytes 786440 | tf_op jit(solution)/shard_map/ppermute | solution.py:14
  634.4 6.4 collective-permute-start.10
  646.5 101.1 %all-reduce.8.cloned.1.call-start = ((), (), s32[]{:S(2)}) async-start(), calls=%async_computation.8 | async-start | bytes 4194304 | tf_op jit(solution)/shard_map/psum | solution.py:80
  754.4 7.1 collective-permute-start.11
  (28 other events, 135.6 us)
Sparse Core Ops, SparseCore 0:
  42.1 38.3 reduce-scatter.3
  85.6 65.6 all-reduce.3
  375.2 27.5 reduce-scatter.5
  407.8 65.5 all-reduce.5
  646.6 30.2 reduce-scatter.7
  681.9 65.5 all-reduce.7
